TPU v7x, 512 devices: a whole 4x4x16 slice. The times are simulated.
512 devices in a mesh: rows: 128 (over z, y, core), grp: 4 (over x).
Axes of the slice: x: 4, y: 4, z: 16, core: 2. Of those that a mesh axis runs over, the one named last changes fastest.
Arguments:
- rhs: float32 [3, 128, 4, 2, 512], P(None, 'rows', 'grp'), may hold values from -6 to 6
- diag_inverse: bfloat16 [3, 128, 4, 512, 512], P(None, 'rows', 'grp'), as said below
- coupling: bfloat16 [3, 128, 4, 512, 512], P(None, 'rows', 'grp'), may hold values from -0.125 to 0.125
- off_block: bfloat16 [2, 128, 4, 512, 512], P(None, 'rows', 'grp'), may hold values from -0.1875 to 0.1875
- off_route: int32 [2, 128, 4], P(None, 'rows', 'grp'), may hold values from 0 to 255, as said below
Outputs:
- solution: float32 [3, 128, 4, 2, 512], P(None, 'rows', 'grp')
Inputs may be any that keep to these rules, and one draw needn't show every extreme that they name: `off_route`: for a block of super-level l the value is s * 128 + t with 0 <= s <= 1 - l: the block belongs to block row t of the same group in super-level l + 1 + s. `diag_inverse`: each matrix is a dominant diagonal plus independent off-diagonal entries.
All inputs are finite; a program needn't handle non-finite values.
Results may differ from a plain program's by a relative error of at most 0.0045.
Values may be sent and summed in bfloat16 or wider, within the bound.
A program may use at most 64 MiB of HBM per device.

v0:
```python
import jax
import jax.numpy as jnp
from jax import lax
from jax.sharding import PartitionSpec as P


def shifted(value, axis, steps):
    count = lax.axis_size(axis)
    first, last = (max(0, -steps), min(count, count - steps))
    return lax.ppermute(value, axis, [(source, source + steps) for source in range(first, last)])


def shards(rhs, diag_inverse, coupling, off_block, off_route):
    highest = lax.Precision.HIGHEST
    levels = rhs.shape[0]
    groups = lax.axis_size("grp")
    rowblocks = lax.axis_size("rows")
    source_all = rhs[:, 0, 0]
    inverse_all = diag_inverse[:, 0, 0]
    coupler_all = coupling[:, 0, 0]
    blocks = off_block[:, 0, 0]
    routes = off_route[:, 0, 0]
    pending = [jnp.zeros(source_all.shape[1:], jnp.float32) for index_value in range(levels)]
    results = []
    for super_level in range(levels):
        source = source_all[super_level] - pending[super_level]
        inverse = inverse_all[super_level].astype(jnp.float32)
        coupler = coupler_all[super_level].astype(jnp.float32)
        solved = jnp.dot(source, inverse, precision=highest)
        for repeat in range(groups - 1):
            before = shifted(solved, "grp", 1)
            solved = jnp.dot(
                source - jnp.dot(before, coupler, precision=highest), inverse, precision=highest
            )
        results.append(solved)
        if super_level < levels - 1:
            contribution = jnp.dot(
                solved.astype(jnp.bfloat16), blocks[super_level], preferred_element_type=jnp.float32
            ).astype(jnp.bfloat16)
            ahead_count = levels - 1 - super_level
            routing = routes[super_level]
            level_skip = routing // rowblocks
            target_row = routing % rowblocks
            one_hot = (jnp.arange(ahead_count, dtype=jnp.int32)[:, None] == level_skip) & (
                jnp.arange(rowblocks, dtype=jnp.int32)[None, :] == target_row
            )
            send_buffer = jnp.where(
                one_hot[:, :, None, None], contribution[None, None], jnp.zeros((), jnp.bfloat16)
            )
            received = lax.all_to_all(send_buffer, "rows", split_axis=1, concat_axis=1, tiled=True)
            arrived = jnp.sum(received.astype(jnp.float32), axis=1)
            for ahead in range(ahead_count):
                pending[super_level + 1 + ahead] = pending[super_level + 1 + ahead] + arrived[ahead]
    return jnp.stack(results, axis=0)[:, None, None]


def solution(mesh):
    return jax.shard_map(
        shards,
        mesh=mesh,
        in_specs=(
            P(None, "rows", "grp", None, None),
            P(None, "rows", "grp", None, None),
            P(None, "rows", "grp", None, None),
            P(None, "rows", "grp", None, None),
            P(None, "rows", "grp"),
        ),
        out_specs=P(None, "rows", "grp", None, None),
        check_vma=False,
    )
```

profile of v0, /device:TPU:36, one launch (start us, length us, event | category | flops | bytes accessed | tf_op | source)
XLA Modules:
  0.0 147.0 jit_solution(16518133358911628956)
XLA Ops:
  0.0 1.5 %fusion.32 = f32[2,512]{1,0:T(2,128)S(1)} fusion(bf16[3,1,1,512,512]{4,3,2,1,0:T(8,128)(2,1)} %param.6, f32[3,1,1,2,512]{4,3,2,1,0:T(2,128)} %param.5), kind=kOutput, calls=%fused_computation.46 | convolution fusion | flops 6291456 | bytes 532480 | tf_op jit(solution)/shard_map/dot_general | solution.py:29
  1.5 3.1 %collective-permute-start = (f32[2,512]{1,0:T(2,128)S(1)}, f32[2,512]{1,0:T(2,128)S(1)}, u32[]{:S(2)}, u32[]{:S(2)}) collective-permute-start(f32[2,512]{1,0:T(2,128)S(1)} %fusion.32), channel_id=1, source_target_pairs={{0,1},{1,2},{2,3},{4,5},{5,6},{6,7},{8,9},{9,10},{10,11},{12,13},{... | collective-permute-start | bytes 12296 | tf_op jit(solution)/shard_map/ppermute | solution.py:10
  4.6 1.4 fusion.71
  8.6 1.4 convolution_subtract_fusion.8
  10.1 1.4 fusion.30
  11.4 1.9 %collective-permute-start.1 = (f32[2,512]{1,0:T(2,128)S(1)}, f32[2,512]{1,0:T(2,128)S(1)}, u32[]{:S(2)}, u32[]{:S(2)}) collective-permute-start(f32[2,512]{1,0:T(2,128)S(1)} %fusion.30), channel_id=1, source_target_pairs={{0,1},{1,2},{2,3},{4,5},{5,6},{6,7},{8,9},{9,10},{10,11},{12,13},{... | collective-permute-start | bytes 12296 | tf_op jit(solution)/shard_map/ppermute | solution.py:10
  13.4 3.6 %collective-permute-done.1 = f32[2,512]{1,0:T(2,128)S(1)} collective-permute-done((f32[2,512]{1,0:T(2,128)S(1)}, f32[2,512]{1,0:T(2,128)S(1)}, u32[]{:S(2)}, u32[]{:S(2)}) %collective-permute-start.1) | collective-permute-done | bytes 4128 | tf_op jit(solution)/shard_map/ppermute | solution.py:10
  16.9 1.3 convolution_subtract_fusion.7
  18.6 1.9 %collective-permute-start.2 = (f32[2,512]{1,0:T(2,128)S(1)}, f32[2,512]{1,0:T(2,128)S(1)}, u32[]{:S(2)}, u32[]{:S(2)}) collective-permute-start(f32[2,512]{1,0:T(2,128)S(1)} %fusion.28), channel_id=1, source_target_pairs={{0,1},{1,2},{2,3},{4,5},{5,6},{6,7},{8,9},{9,10},{10,11},{12,13},{... | collective-permute-start | bytes 12296 | tf_op jit(solution)/shard_map/ppermute | solution.py:10
  20.6 3.5 %collective-permute-done.2 = f32[2,512]{1,0:T(2,128)S(1)} collective-permute-done((f32[2,512]{1,0:T(2,128)S(1)}, f32[2,512]{1,0:T(2,128)S(1)}, u32[]{:S(2)}, u32[]{:S(2)}) %collective-permute-start.2) | collective-permute-done | bytes 4128 | tf_op jit(solution)/shard_map/ppermute | solution.py:10
  24.1 1.3 convolution_subtract_fusion.6
  26.6 52.1 %all_to_all.10 = bf16[2,128,2,512]{3,2,0,1:T(2,128)(2,1)S(1)} all-to-all(bf16[2,128,2,512]{3,2,0,1:T(2,128)(2,1)S(1)} %broadcast_select_fusion), channel_id=1, replica_groups=mesh['rows'=128,'grp'=4] {'rows'}, dimensions={1} | all-to-all | bytes 1048576 | tf_op jit(solution)/shard_map/all_to_all | solution.py:50
  79.5 1.9 %collective-permute-start.3 = (f32[2,512]{1,0:T(2,128)S(1)}, f32[2,512]{1,0:T(2,128)S(1)}, u32[]{:S(2)}, u32[]{:S(2)}) collective-permute-start(f32[2,512]{1,0:T(2,128)S(1)} %fusion.20), channel_id=1, source_target_pairs={{0,1},{1,2},{2,3},{4,5},{5,6},{6,7},{8,9},{9,10},{10,11},{12,13},{... | collective-permute-start | bytes 12296 | tf_op jit(solution)/shard_map/ppermute | solution.py:10
  81.4 3.6 %collective-permute-done.3 = f32[2,512]{1,0:T(2,128)S(1)} collective-permute-done((f32[2,512]{1,0:T(2,128)S(1)}, f32[2,512]{1,0:T(2,128)S(1)}, u32[]{:S(2)}, u32[]{:S(2)}) %collective-permute-start.3) | collective-permute-done | bytes 4128 | tf_op jit(solution)/shard_map/ppermute | solution.py:10
  85.6 2.0 %collective-permute-start.4 = (f32[2,512]{1,0:T(2,128)S(1)}, f32[2,512]{1,0:T(2,128)S(1)}, u32[]{:S(2)}, u32[]{:S(2)}) collective-permute-start(f32[2,512]{1,0:T(2,128)S(1)} %fusion.18), channel_id=1, source_target_pairs={{0,1},{1,2},{2,3},{4,5},{5,6},{6,7},{8,9},{9,10},{10,11},{12,13},{... | collective-permute-start | bytes 12296 | tf_op jit(solution)/shard_map/ppermute | solution.py:10
  91.8 2.0 %collective-permute-start.5 = (f32[2,512]{1,0:T(2,128)S(1)}, f32[2,512]{1,0:T(2,128)S(1)}, u32[]{:S(2)}, u32[]{:S(2)}) collective-permute-start(f32[2,512]{1,0:T(2,128)S(1)} %fusion.16), channel_id=1, source_target_pairs={{0,1},{1,2},{2,3},{4,5},{5,6},{6,7},{8,9},{9,10},{10,11},{12,13},{... | collective-permute-start | bytes 12296 | tf_op jit(solution)/shard_map/ppermute | solution.py:10
  93.7 3.5 %collective-permute-done.5 = f32[2,512]{1,0:T(2,128)S(1)} collective-permute-done((f32[2,512]{1,0:T(2,128)S(1)}, f32[2,512]{1,0:T(2,128)S(1)}, u32[]{:S(2)}, u32[]{:S(2)}) %collective-permute-start.5) | collective-permute-done | bytes 4128 | tf_op jit(solution)/shard_map/ppermute | solution.py:10
  98.4 29.1 %all_to_all.11 = bf16[1,128,2,512]{3,2,0,1:T(2,128)(2,1)S(1)} all-to-all(bf16[1,128,2,512]{3,2,0,1:T(2,128)(2,1)S(1)} %broadcast_select_fusion.1), channel_id=1, replica_groups=mesh['rows'=128,'grp'=4] {'rows'}, dimensions={1} | all-to-all | bytes 524288 | tf_op jit(solution)/shard_map/all_to_all | solution.py:50
  128.0 1.9 %collective-permute-start.6 = (f32[2,512]{1,0:T(2,128)S(1)}, f32[2,512]{1,0:T(2,128)S(1)}, u32[]{:S(2)}, u32[]{:S(2)}) collective-permute-start(f32[2,512]{1,0:T(2,128)S(1)} %fusion.8), channel_id=1, source_target_pairs={{0,1},{1,2},{2,3},{4,5},{5,6},{6,7},{8,9},{9,10},{10,11},{12,13},{... | collective-permute-start | bytes 12296 | tf_op jit(solution)/shard_map/ppermute | solution.py:10
  130.0 3.6 %collective-permute-done.6 = f32[2,512]{1,0:T(2,128)S(1)} collective-permute-done((f32[2,512]{1,0:T(2,128)S(1)}, f32[2,512]{1,0:T(2,128)S(1)}, u32[]{:S(2)}, u32[]{:S(2)}) %collective-permute-start.6) | collective-permute-done | bytes 4128 | tf_op jit(solution)/shard_map/ppermute | solution.py:10
  134.2 1.9 %collective-permute-start.7 = (f32[2,512]{1,0:T(2,128)S(1)}, f32[2,512]{1,0:T(2,128)S(1)}, u32[]{:S(2)}, u32[]{:S(2)}) collective-permute-start(f32[2,512]{1,0:T(2,128)S(1)} %fusion.6), channel_id=1, source_target_pairs={{0,1},{1,2},{2,3},{4,5},{5,6},{6,7},{8,9},{9,10},{10,11},{12,13},{... | collective-permute-start | bytes 12296 | tf_op jit(solution)/shard_map/ppermute | solution.py:10
  136.1 3.6 %collective-permute-done.7 = f32[2,512]{1,0:T(2,128)S(1)} collective-permute-done((f32[2,512]{1,0:T(2,128)S(1)}, f32[2,512]{1,0:T(2,128)S(1)}, u32[]{:S(2)}, u32[]{:S(2)}) %collective-permute-start.7) | collective-permute-done | bytes 4128 | tf_op jit(solution)/shard_map/ppermute | solution.py:10
  140.3 1.9 %collective-permute-start.8 = (f32[2,512]{1,0:T(2,128)S(1)}, f32[2,512]{1,0:T(2,128)S(1)}, u32[]{:S(2)}, u32[]{:S(2)}) collective-permute-start(f32[2,512]{1,0:T(2,128)S(1)} %fusion.4), channel_id=1, source_target_pairs={{0,1},{1,2},{2,3},{4,5},{5,6},{6,7},{8,9},{9,10},{10,11},{12,13},{... | collective-permute-start | bytes 12296 | tf_op jit(solution)/shard_map/ppermute | solution.py:10
  142.2 3.6 %collective-permute-done.8 = f32[2,512]{1,0:T(2,128)S(1)} collective-permute-done((f32[2,512]{1,0:T(2,128)S(1)}, f32[2,512]{1,0:T(2,128)S(1)}, u32[]{:S(2)}, u32[]{:S(2)}) %collective-permute-start.8) | collective-permute-done | bytes 4128 | tf_op jit(solution)/shard_map/ppermute | solution.py:10
  (40 shorter events, 8.8 us)
Async XLA Ops:
  0.0 18.3 %copy-start = (bf16[3,1,1,512,512]{4,3,2,1,0:T(8,128)(2,1)S(1)}, bf16[3,1,1,512,512]{4,3,2,1,0:T(8,128)(2,1)}, u32[]{:S(2)}) copy-start(bf16[3,1,1,512,512]{4,3,2,1,0:T(8,128)(2,1)} %param.6) | copy-start | bytes 4718596
  0.0 16.9 %copy-start.4 = (f32[3,1,1,2,512]{4,3,2,1,0:T(2,128)S(1)}, f32[3,1,1,2,512]{4,3,2,1,0:T(2,128)}, u32[]{:S(2)}) copy-start(f32[3,1,1,2,512]{4,3,2,1,0:T(2,128)} %param.5) | copy-start | bytes 36868
  1.5 7.1 %collective-permute-start = (f32[2,512]{1,0:T(2,128)S(1)}, f32[2,512]{1,0:T(2,128)S(1)}, u32[]{:S(2)}, u32[]{:S(2)}) collective-permute-start(f32[2,512]{1,0:T(2,128)S(1)} %fusion.32), channel_id=1, source_target_pairs={{0,1},{1,2},{2,3},{4,5},{5,6},{6,7},{8,9},{9,10},{10,11},{12,13},{... | collective-permute-start | bytes 12296 | tf_op jit(solution)/shard_map/ppermute | solution.py:10
  8.6 17.2 %copy-start.2 = (bf16[2,1,1,512,512]{4,3,2,1,0:T(8,128)(2,1)S(1)}, bf16[2,1,1,512,512]{4,3,2,1,0:T(8,128)(2,1)}, u32[]{:S(2)}) copy-start(bf16[2,1,1,512,512]{4,3,2,1,0:T(8,128)(2,1)} %param.8) | copy-start | bytes 3145732
  11.4 5.5 %collective-permute-start.1 = (f32[2,512]{1,0:T(2,128)S(1)}, f32[2,512]{1,0:T(2,128)S(1)}, u32[]{:S(2)}, u32[]{:S(2)}) collective-permute-start(f32[2,512]{1,0:T(2,128)S(1)} %fusion.30), channel_id=1, source_target_pairs={{0,1},{1,2},{2,3},{4,5},{5,6},{6,7},{8,9},{9,10},{10,11},{12,13},{... | collective-permute-start | bytes 12296 | tf_op jit(solution)/shard_map/ppermute | solution.py:10
  18.6 5.5 %collective-permute-start.2 = (f32[2,512]{1,0:T(2,128)S(1)}, f32[2,512]{1,0:T(2,128)S(1)}, u32[]{:S(2)}, u32[]{:S(2)}) collective-permute-start(f32[2,512]{1,0:T(2,128)S(1)} %fusion.28), channel_id=1, source_target_pairs={{0,1},{1,2},{2,3},{4,5},{5,6},{6,7},{8,9},{9,10},{10,11},{12,13},{... | collective-permute-start | bytes 12296 | tf_op jit(solution)/shard_map/ppermute | solution.py:10
  25.8 59.2 %copy-start.1 = (bf16[3,1,1,512,512]{4,3,2,1,0:T(8,128)(2,1)S(1)}, bf16[3,1,1,512,512]{4,3,2,1,0:T(8,128)(2,1)}, u32[]{:S(2)}) copy-start(bf16[3,1,1,512,512]{4,3,2,1,0:T(8,128)(2,1)} %param.7) | copy-start | bytes 4718596
  79.5 5.5 %collective-permute-start.3 = (f32[2,512]{1,0:T(2,128)S(1)}, f32[2,512]{1,0:T(2,128)S(1)}, u32[]{:S(2)}, u32[]{:S(2)}) collective-permute-start(f32[2,512]{1,0:T(2,128)S(1)} %fusion.20), channel_id=1, source_target_pairs={{0,1},{1,2},{2,3},{4,5},{5,6},{6,7},{8,9},{9,10},{10,11},{12,13},{... | collective-permute-start | bytes 12296 | tf_op jit(solution)/shard_map/ppermute | solution.py:10
  85.6 5.5 %collective-permute-start.4 = (f32[2,512]{1,0:T(2,128)S(1)}, f32[2,512]{1,0:T(2,128)S(1)}, u32[]{:S(2)}, u32[]{:S(2)}) collective-permute-start(f32[2,512]{1,0:T(2,128)S(1)} %fusion.18), channel_id=1, source_target_pairs={{0,1},{1,2},{2,3},{4,5},{5,6},{6,7},{8,9},{9,10},{10,11},{12,13},{... | collective-permute-start | bytes 12296 | tf_op jit(solution)/shard_map/ppermute | solution.py:10
  90.1 7.8 %copy-start.3 = (bf16[2,1,1,512,512]{4,3,2,1,0:T(8,128)(2,1)S(1)}, bf16[2,1,1,512,512]{4,3,2,1,0:T(8,128)(2,1)}, u32[]{:S(2)}) copy-start(bf16[2,1,1,512,512]{4,3,2,1,0:T(8,128)(2,1)} %param.8) | copy-start | bytes 3145732
  91.8 5.5 %collective-permute-start.5 = (f32[2,512]{1,0:T(2,128)S(1)}, f32[2,512]{1,0:T(2,128)S(1)}, u32[]{:S(2)}, u32[]{:S(2)}) collective-permute-start(f32[2,512]{1,0:T(2,128)S(1)} %fusion.16), channel_id=1, source_target_pairs={{0,1},{1,2},{2,3},{4,5},{5,6},{6,7},{8,9},{9,10},{10,11},{12,13},{... | collective-permute-start | bytes 12296 | tf_op jit(solution)/shard_map/ppermute | solution.py:10
  128.0 5.5 %collective-permute-start.6 = (f32[2,512]{1,0:T(2,128)S(1)}, f32[2,512]{1,0:T(2,128)S(1)}, u32[]{:S(2)}, u32[]{:S(2)}) collective-permute-start(f32[2,512]{1,0:T(2,128)S(1)} %fusion.8), channel_id=1, source_target_pairs={{0,1},{1,2},{2,3},{4,5},{5,6},{6,7},{8,9},{9,10},{10,11},{12,13},{... | collective-permute-start | bytes 12296 | tf_op jit(solution)/shard_map/ppermute | solution.py:10
  134.2 5.5 %collective-permute-start.7 = (f32[2,512]{1,0:T(2,128)S(1)}, f32[2,512]{1,0:T(2,128)S(1)}, u32[]{:S(2)}, u32[]{:S(2)}) collective-permute-start(f32[2,512]{1,0:T(2,128)S(1)} %fusion.6), channel_id=1, source_target_pairs={{0,1},{1,2},{2,3},{4,5},{5,6},{6,7},{8,9},{9,10},{10,11},{12,13},{... | collective-permute-start | bytes 12296 | tf_op jit(solution)/shard_map/ppermute | solution.py:10
  140.3 5.5 %collective-permute-start.8 = (f32[2,512]{1,0:T(2,128)S(1)}, f32[2,512]{1,0:T(2,128)S(1)}, u32[]{:S(2)}, u32[]{:S(2)}) collective-permute-start(f32[2,512]{1,0:T(2,128)S(1)} %fusion.4), channel_id=1, source_target_pairs={{0,1},{1,2},{2,3},{4,5},{5,6},{6,7},{8,9},{9,10},{10,11},{12,13},{... | collective-permute-start | bytes 12296 | tf_op jit(solution)/shard_map/ppermute | solution.py:10
where the time goes:
time: 148 us; the launch traced here: 147 us
  blocking collectives  81.2 us (55%)
  waiting for transfers between devices  25.8 us (17%)
  starting transfers between devices  18.6 us (13%)
  matrix products  12.3 us (8%)
  between operations  5.31 us (4%)
  other arithmetic  2.42 us (2%)
    all_to_all x2, blocking collectives, shards(): lax.all_to_all(send_buffer, 'rows', split_axis=1, concat_axis=1, tiled=True)  81.2 us
    ppermute x9, waiting for transfers between devices, shifted(): lax.ppermute(value, axis, [(source, source + steps) for source in range(f...  25.8 us
    ppermute x9, starting transfers between devices, shifted(): lax.ppermute(value, axis, [(source, source + steps) for source in range(f...  18.6 us
    dot_general x9, matrix products, shards(): jnp.dot(before, coupler, precision=highest)  5.96 us
    dot_general x9, matrix products, shards(): jnp.dot(source - jnp.dot(before, coupler, precision=highest), inverse, pr...  3.9 us
  transfers between devices with their start and end apart: 9, of which 8 were waited for; matrix products, arithmetic and copies ran while one was open for 1% of the time, Pallas kernels for 0%

commit v1 on v0

v1 whole, which is shorter than its diff:
```python
import functools

import jax
import jax.numpy as jnp
from jax import lax
from jax.experimental import pallas as pl
from jax.experimental.pallas import tpu as pltpu
from jax.sharding import PartitionSpec as P

INNER = 8
MESH = pl.DeviceIdType.MESH


def far_first(count):
    return sorted(range(1, count), key=lambda offset: -min(offset, count - offset))


def kernel(
    outer, groups, rhs_hbm, inverse_hbm, coupler_hbm, block_hbm, route_hbm, out_ref,
    rhs, inverse, coupler, block, route, code, codes, solved, before, sent, zland, held, part, yland,
    in_sem, code_send, code_recv, x_send, x_recv, z_send, z_recv, y_send, y_recv,
):
    levels = rhs.shape[0]
    rowblocks = outer * INNER
    row = lax.axis_index("rows")
    grp = lax.axis_index("grp")
    zpos = row // INNER
    spot = row % INNER

    def z_peer(offset):
        return {"rows": ((zpos + offset) % outer) * INNER + spot}

    def y_peer(offset):
        return {"rows": zpos * INNER + (spot + offset) % INNER}

    barrier = pltpu.get_barrier_semaphore()
    for offset in far_first(outer):
        pl.semaphore_signal(barrier, inc=1, device_id=z_peer(offset), device_id_type=MESH)
    for offset in far_first(INNER):
        pl.semaphore_signal(barrier, inc=1, device_id=y_peer(offset), device_id_type=MESH)

    left = {"grp": (grp + groups - 1) % groups}
    pl.semaphore_signal(barrier, inc=1, device_id=left, device_id_type=MESH)

    loads = [pltpu.make_async_copy(rhs_hbm, rhs, in_sem.at[0]), pltpu.make_async_copy(route_hbm, route, in_sem.at[1])]
    index = 2
    matrices = []
    for level in range(levels):
        entry = {}
        for name, source, target in (("D", inverse_hbm, inverse), ("E", block_hbm, block), ("C", coupler_hbm, coupler)):
            if name == "E" and level == levels - 1:
                continue
            copy = pltpu.make_async_copy(source.at[level], target.at[level], in_sem.at[index])
            index += 1
            loads.append(copy)
            entry[name] = copy
        matrices.append(entry)
    for copy in loads:
        copy.start()

    quarter = lax.broadcasted_iota(jnp.int32, (8, 128), 0) // 2

    def spread(v8):
        return jnp.concatenate([jnp.where(quarter == j, v8, 0.0) for j in range(4)], axis=1)

    def fold(p):
        q = p + pltpu.roll(p, 4, 0)
        q = q + pltpu.roll(q, 2, 0)
        out = q[:, 0:128]
        for j in range(1, 4):
            out = jnp.where(quarter == j, q[:, 128 * j : 128 * (j + 1)], out)
        return out

    def product(v8, matrix):
        wide = spread(v8)
        low = wide - wide.astype(jnp.bfloat16).astype(jnp.float32)
        stack = jnp.concatenate([wide, low], axis=0).astype(jnp.bfloat16)
        p = jnp.dot(stack, matrix, preferred_element_type=jnp.float32)
        return fold(p[0:8] + p[8:16])

    def rounded_product(v8, matrix):
        wide = spread(v8)
        stack = jnp.concatenate([wide, jnp.zeros_like(wide)], axis=0).astype(jnp.bfloat16)
        p = jnp.dot(stack, matrix, preferred_element_type=jnp.float32)
        return fold(p[0:8])

    def contribute(level):
        sent[level] = rounded_product(solved[level], block[level]).astype(jnp.bfloat16)

    loads[0].wait()
    loads[1].wait()
    both = route[0, 0] + 256 * route[0, 1]
    code[...] = jnp.full((1, 128), both, jnp.int32)
    matrices[0]["D"].wait()
    solved[0] = product(rhs[0], inverse[0])
    matrices[0]["E"].wait()
    contribute(0)
    matrices[0]["C"].wait()

    pl.semaphore_wait(barrier, outer - 1 + INNER - 1 + 1)

    def code_copy(offset):
        return pltpu.make_async_remote_copy(
            src_ref=code, dst_ref=codes.at[offset], send_sem=code_send, recv_sem=code_recv,
            device_id=z_peer(offset), device_id_type=MESH,
        )

    def x_copy(level):
        return pltpu.make_async_remote_copy(
            src_ref=solved.at[level], dst_ref=before.at[level], send_sem=x_send.at[level], recv_sem=x_recv.at[level],
            device_id={"grp": grp + 1}, device_id_type=MESH,
        )

    def z_copy(level, offset):
        return pltpu.make_async_remote_copy(
            src_ref=sent.at[level], dst_ref=zland.at[level, offset], send_sem=z_send.at[level], recv_sem=z_recv.at[level],
            device_id=z_peer(offset), device_id_type=MESH,
        )

    def y_copy(level, offset):
        return pltpu.make_async_remote_copy(
            src_ref=part.at[level, offset], dst_ref=yland.at[level, offset], send_sem=y_send.at[level],
            recv_sem=y_recv.at[level], device_id=y_peer(offset), device_id_type=MESH,
        )

    def bulk_wait(ref, sem):
        pltpu.make_async_copy(ref, ref, sem).wait()

    z_order, y_order = far_first(outer), far_first(INNER)

    for level in range(levels):
        if level > 0:
            matrices[level]["D"].wait()
            matrices[level]["C"].wait()
            if level < levels - 1:
                matrices[level]["E"].wait()
            bulk_wait(yland.at[level - 1, pl.ds(1, INNER - 1)], y_recv.at[level - 1])
            incoming = part[level - 1, 0]
            for offset in range(1, INNER):
                incoming = incoming + yland[level - 1, offset]
            solved[level] = product(rhs[level] - incoming, inverse[level])

        @pl.when(grp > 0)
        def _():
            bulk_wait(before.at[level], x_recv.at[level])
            solved[level] = solved[level] - product(product(before[level], coupler[level]), inverse[level])

        @pl.when(grp < groups - 1)
        def _():
            x_copy(level).start()

        if level == levels - 1:
            break
        if level == 0:
            @pl.when(grp > 0)
            def _():
                contribute(0)
        else:
            contribute(level)
        for offset in z_order:
            z_copy(level, offset).start()
        if level == 0:
            for offset in z_order:
                code_copy(offset).start()
            codes[0] = code[...]
            bulk_wait(codes.at[pl.ds(1, outer - 1)], code_recv)
        bulk_wait(zland.at[level, pl.ds(1, outer - 1)], z_recv.at[level])

        arrived = [sent[level].astype(jnp.float32)]
        arrived += [zland[level, offset].astype(jnp.float32) for offset in range(1, outer)]
        marks = [jnp.broadcast_to(codes[offset], (8, 128)) for offset in range(outer)]
        marks = [(mark // 256 if level else mark % 256) for mark in marks]

        def gathered(target):
            terms = [jnp.where(mark == target, value, 0.0) for mark, value in zip(marks, arrived)]
            while len(terms) > 1:
                terms = [terms[i] + terms[i + 1] for i in range(0, len(terms), 2)]
            return terms[0]

        for offset in y_order + [0]:
            target = zpos * INNER + (spot + offset) % INNER
            total = gathered(target)
            if level > 0:
                total = total + held[offset]
            part[level, offset] = total
            if offset:
                y_copy(level, offset).start()
        if level == 0:
            for offset in range(INNER):
                held[offset] = gathered(zpos * INNER + (spot + offset) % INNER + rowblocks)

    out_ref[...] = solved[...]

    bulk_wait(codes.at[pl.ds(1, outer - 1)], code_send)
    for level in range(levels - 1):
        bulk_wait(zland.at[level, pl.ds(1, outer - 1)], z_send.at[level])
        bulk_wait(part.at[level, pl.ds(1, INNER - 1)], y_send.at[level])

    @pl.when(grp < groups - 1)
    def _():
        for level in range(levels):
            bulk_wait(solved.at[level], x_send.at[level])


def shards(rhs, diag_inverse, coupling, off_block, off_route):
    groups = lax.axis_size("grp")
    outer = lax.axis_size("rows") // INNER
    levels, size = rhs.shape[0], rhs.shape[-1]
    assert levels == 3 and rhs.shape[-2:] == (2, 512)
    rows8 = rhs[:, 0, 0].reshape(levels, 2, 4, 128).transpose(0, 2, 1, 3).reshape(levels, 8, 128)
    hbm = pl.BlockSpec(memory_space=pl.ANY)
    dma = pltpu.SemaphoreType.DMA
    out = pl.pallas_call(
        functools.partial(kernel, outer, groups),
        out_shape=jax.ShapeDtypeStruct((levels, 8, 128), jnp.float32),
        in_specs=[hbm] * 5,
        out_specs=pl.BlockSpec(memory_space=pltpu.VMEM),
        scratch_shapes=[
            pltpu.VMEM((levels, 8, 128), jnp.float32),
            pltpu.VMEM((levels, size, size), jnp.bfloat16),
            pltpu.VMEM((levels, size, size), jnp.bfloat16),
            pltpu.VMEM((levels - 1, size, size), jnp.bfloat16),
            pltpu.SMEM((1, levels - 1), jnp.int32),
            pltpu.VMEM((1, 128), jnp.int32),
            pltpu.VMEM((outer, 1, 128), jnp.int32),
            pltpu.VMEM((levels, 8, 128), jnp.float32),
            pltpu.VMEM((levels, 8, 128), jnp.float32),
            pltpu.VMEM((levels - 1, 8, 128), jnp.bfloat16),
            pltpu.VMEM((levels - 1, outer, 8, 128), jnp.bfloat16),
            pltpu.VMEM((INNER, 8, 128), jnp.float32),
            pltpu.VMEM((levels - 1, INNER, 8, 128), jnp.float32),
            pltpu.VMEM((levels - 1, INNER, 8, 128), jnp.float32),
            dma((2 + 3 * levels - 1,)),
            dma, dma,
            dma((levels,)), dma((levels,)),
            dma((levels - 1,)), dma((levels - 1,)),
            dma((levels - 1,)), dma((levels - 1,)),
        ],
        compiler_params=pltpu.CompilerParams(collective_id=0, has_side_effects=True),
    )(rows8, diag_inverse[:, 0, 0], coupling[:, 0, 0], off_block[:, 0, 0], off_route[:, 0].T)
    out = out.reshape(levels, 4, 2, 128).transpose(0, 2, 1, 3).reshape(levels, 2, size)
    return out[:, None, None]


def solution(mesh):
    return jax.shard_map(
        shards,
        mesh=mesh,
        in_specs=(
            P(None, "rows", "grp", None, None),
            P(None, "rows", "grp", None, None),
            P(None, "rows", "grp", None, None),
            P(None, "rows", "grp", None, None),
            P(None, "rows", "grp"),
        ),
        out_specs=P(None, "rows", "grp", None, None),
        check_vma=False,
    )
```

time: 148 us -> 49.1 us (0.33)
  the two profiles are of different devices: /device:TPU:36 before, /device:TPU:6 now
where the time goes in v1:
time: 49.1 us; the launch traced here: 48.6 us
  Pallas kernels  47.2 us (96%)
  local copies, waits for them, and re-layouts  1.31 us (3%)
    pallas_call x1, Pallas kernels, shards(): pl.pallas_call(functools.partial(kernel, outer, groups), out_shape=jax.Sh...  47.2 us
    unnamed x1, local copies, waits for them, and re-layouts  1.31 us

profile of v1, /device:TPU:6, one launch (start us, length us, event | category | flops | bytes accessed | tf_op | source)
XLA Modules:
  0.0 48.6 jit_solution(6102901257677768886)
XLA Ops:
  0.0 47.2 %shard_map.55 = f32[3,8,128]{2,1,0:T(8,128)} custom-call(f32[3,8,128]{2,1,0:T(8,128)} %bitcast.18, bf16[3,512,512]{2,1,0:T(8,128)(2,1)} %bitcast.14, bf16[3,512,512]{2,1,0:T(8,128)(2,1)} %bitcast.15, bf16[2,512,512]{2,1,0:T(8,128)(2,1)} %bitcast.16, s32[1,2]{1,0:T(1,128)} %bitcast.19), custom_call_target="tpu_custom_call" | custom-call | tf_op jit(solution)/shard_map/pallas_call | solution.py:213
  47.2 1.3 %copy.9 = f32[3,1,1,2,512]{4,3,2,1,0:T(2,128)} copy(f32[3,1,1,2,512]{4,3,2,1,0:T(2,128)} %bitcast.17) | data formatting | bytes 24576

commit v2 on v1

--- a/solution.py
+++ b/solution.py
@@ -17,8 +17,8 @@
 
 def kernel(
     outer, groups, rhs_hbm, inverse_hbm, coupler_hbm, block_hbm, route_hbm, out_ref,
-    rhs, inverse, coupler, block, route, code, codes, solved, before, sent, zland, held, part, yland,
-    in_sem, code_send, code_recv, x_send, x_recv, z_send, z_recv, y_send, y_recv,
+    rhs, inverse, coupler, block, route, code, codes, solved, before, sent, yland, held, part, zland,
+    in_sem, meet, code_send, code_recv, x_send, x_recv, y_send, y_recv, z_send, z_recv,
 ):
     levels = rhs.shape[0]
     rowblocks = outer * INNER
@@ -34,11 +34,10 @@
         return {"rows": zpos * INNER + (spot + offset) % INNER}
 
     barrier = pltpu.get_barrier_semaphore()
-    for offset in far_first(outer):
+    for offset in (1, outer - 1):
         pl.semaphore_signal(barrier, inc=1, device_id=z_peer(offset), device_id_type=MESH)
     for offset in far_first(INNER):
         pl.semaphore_signal(barrier, inc=1, device_id=y_peer(offset), device_id_type=MESH)
-
     left = {"grp": (grp + groups - 1) % groups}
     pl.semaphore_signal(barrier, inc=1, device_id=left, device_id_type=MESH)
 
@@ -55,7 +54,8 @@
             loads.append(copy)
             entry[name] = copy
         matrices.append(entry)
-    for copy in loads:
+    first = loads[:5]
+    for copy in first:
         copy.start()
 
     quarter = lax.broadcasted_iota(jnp.int32, (8, 128), 0) // 2
@@ -92,17 +92,30 @@
     both = route[0, 0] + 256 * route[0, 1]
     code[...] = jnp.full((1, 128), both, jnp.int32)
     matrices[0]["D"].wait()
+    for copy in loads[5:]:
+        copy.start()
     solved[0] = product(rhs[0], inverse[0])
     matrices[0]["E"].wait()
     contribute(0)
     matrices[0]["C"].wait()
 
-    pl.semaphore_wait(barrier, outer - 1 + INNER - 1 + 1)
+    pl.semaphore_wait(barrier, 2 + INNER - 1 + 1)
+
+    rounds = max(1, (outer // 2 - 1).bit_length())
+
+    def greet(step):
+        for offset in (2**step, outer - 2**step):
+            pl.semaphore_signal(meet.at[step], inc=1, device_id=z_peer(offset), device_id_type=MESH)
+
+    def met(step):
+        pl.semaphore_wait(meet.at[step], 2)
+
+    greet(0)
 
     def code_copy(offset):
         return pltpu.make_async_remote_copy(
             src_ref=code, dst_ref=codes.at[offset], send_sem=code_send, recv_sem=code_recv,
-            device_id=z_peer(offset), device_id_type=MESH,
+            device_id=y_peer(offset), device_id_type=MESH,
         )
 
     def x_copy(level):
@@ -111,22 +124,35 @@
             device_id={"grp": grp + 1}, device_id_type=MESH,
         )
 
+    def y_copy(level, offset):
+        return pltpu.make_async_remote_copy(
+            src_ref=sent.at[level], dst_ref=yland.at[level, offset], send_sem=y_send.at[level],
+            recv_sem=y_recv.at[level], device_id=y_peer(offset), device_id_type=MESH,
+        )
+
     def z_copy(level, offset):
         return pltpu.make_async_remote_copy(
-            src_ref=sent.at[level], dst_ref=zland.at[level, offset], send_sem=z_send.at[level], recv_sem=z_recv.at[level],
-            device_id=z_peer(offset), device_id_type=MESH,
-        )
-
-    def y_copy(level, offset):
-        return pltpu.make_async_remote_copy(
-            src_ref=part.at[level, offset], dst_ref=yland.at[level, offset], send_sem=y_send.at[level],
-            recv_sem=y_recv.at[level], device_id=y_peer(offset), device_id_type=MESH,
+            src_ref=part.at[level, offset], dst_ref=zland.at[level, offset], send_sem=z_send.at[level],
+            recv_sem=z_recv.at[level], device_id=z_peer(offset), device_id_type=MESH,
         )
 
     def bulk_wait(ref, sem):
         pltpu.make_async_copy(ref, ref, sem).wait()
 
     z_order, y_order = far_first(outer), far_first(INNER)
+
+    def scatter(level):
+        for offset in y_order:
+            y_copy(level, offset).start()
+
+    for offset in y_order:
+        code_copy(offset).start()
+    codes[0] = code[...]
+
+    def total_of(terms):
+        while len(terms) > 1:
+            terms = [terms[i] + terms[i + 1] for i in range(0, len(terms) - 1, 2)] + terms[len(terms) & ~1 :]
+        return terms[0]
 
     for level in range(levels):
         if level > 0:
@@ -134,67 +160,79 @@
             matrices[level]["C"].wait()
             if level < levels - 1:
                 matrices[level]["E"].wait()
-            bulk_wait(yland.at[level - 1, pl.ds(1, INNER - 1)], y_recv.at[level - 1])
-            incoming = part[level - 1, 0]
-            for offset in range(1, INNER):
-                incoming = incoming + yland[level - 1, offset]
+            bulk_wait(zland.at[level - 1, pl.ds(1, outer - 1)], z_recv.at[level - 1])
+            incoming = total_of(
+                [part[level - 1, 0].astype(jnp.float32)]
+                + [zland[level - 1, offset].astype(jnp.float32) for offset in range(1, outer)]
+            )
             solved[level] = product(rhs[level] - incoming, inverse[level])
+        else:
+            @pl.when(grp == 0)
+            def _():
+                x_copy(0).start()
+                scatter(0)
+
+            met(0)
+            if rounds > 1:
+                greet(1)
 
         @pl.when(grp > 0)
         def _():
             bulk_wait(before.at[level], x_recv.at[level])
             solved[level] = solved[level] - product(product(before[level], coupler[level]), inverse[level])
 
-        @pl.when(grp < groups - 1)
-        def _():
-            x_copy(level).start()
+            @pl.when(grp < groups - 1)
+            def _():
+                x_copy(level).start()
+
+            if level == 0:
+                contribute(0)
+                scatter(0)
+
+        if level > 0:
+            @pl.when(grp == 0)
+            def _():
+                x_copy(level).start()
 
         if level == levels - 1:
             break
-        if level == 0:
-            @pl.when(grp > 0)
-            def _():
-                contribute(0)
+        if level > 0:
+            contribute(level)
+            scatter(level)
         else:
-            contribute(level)
-        for offset in z_order:
-            z_copy(level, offset).start()
-        if level == 0:
-            for offset in z_order:
-                code_copy(offset).start()
-            codes[0] = code[...]
-            bulk_wait(codes.at[pl.ds(1, outer - 1)], code_recv)
-        bulk_wait(zland.at[level, pl.ds(1, outer - 1)], z_recv.at[level])
+            for step in range(1, rounds):
+                met(step)
+                if step + 1 < rounds:
+                    greet(step + 1)
+            bulk_wait(codes.at[pl.ds(1, INNER - 1)], code_recv)
+        bulk_wait(yland.at[level, pl.ds(1, INNER - 1)], y_recv.at[level])
 
         arrived = [sent[level].astype(jnp.float32)]
-        arrived += [zland[level, offset].astype(jnp.float32) for offset in range(1, outer)]
-        marks = [jnp.broadcast_to(codes[offset], (8, 128)) for offset in range(outer)]
+        arrived += [yland[level, offset].astype(jnp.float32) for offset in range(1, INNER)]
+        marks = [jnp.broadcast_to(codes[offset], (8, 128)) for offset in range(INNER)]
         marks = [(mark // 256 if level else mark % 256) for mark in marks]
 
         def gathered(target):
-            terms = [jnp.where(mark == target, value, 0.0) for mark, value in zip(marks, arrived)]
-            while len(terms) > 1:
-                terms = [terms[i] + terms[i + 1] for i in range(0, len(terms), 2)]
-            return terms[0]
-
-        for offset in y_order + [0]:
-            target = zpos * INNER + (spot + offset) % INNER
+            return total_of([jnp.where(mark == target, value, 0.0) for mark, value in zip(marks, arrived)])
+
+        for offset in z_order + [0]:
+            target = ((zpos + offset) % outer) * INNER + spot
             total = gathered(target)
             if level > 0:
                 total = total + held[offset]
-            part[level, offset] = total
+            part[level, offset] = total.astype(jnp.bfloat16)
             if offset:
-                y_copy(level, offset).start()
+                z_copy(level, offset).start()
         if level == 0:
-            for offset in range(INNER):
-                held[offset] = gathered(zpos * INNER + (spot + offset) % INNER + rowblocks)
+            for offset in range(outer):
+                held[offset] = gathered(((zpos + offset) % outer) * INNER + spot + rowblocks)
 
     out_ref[...] = solved[...]
 
-    bulk_wait(codes.at[pl.ds(1, outer - 1)], code_send)
+    bulk_wait(codes.at[pl.ds(1, INNER - 1)], code_send)
     for level in range(levels - 1):
+        bulk_wait(yland.at[level, pl.ds(1, INNER - 1)], y_send.at[level])
         bulk_wait(zland.at[level, pl.ds(1, outer - 1)], z_send.at[level])
-        bulk_wait(part.at[level, pl.ds(1, INNER - 1)], y_send.at[level])
 
     @pl.when(grp < groups - 1)
     def _():
@@ -212,7 +250,7 @@
     dma = pltpu.SemaphoreType.DMA
     out = pl.pallas_call(
         functools.partial(kernel, outer, groups),
-        out_shape=jax.ShapeDtypeStruct((levels, 8, 128), jnp.float32),
+        out_shape=pltpu.VMEM((levels, 8, 128), jnp.float32),
         in_specs=[hbm] * 5,
         out_specs=pl.BlockSpec(memory_space=pltpu.VMEM),
         scratch_shapes=[
@@ -222,15 +260,16 @@
             pltpu.VMEM((levels - 1, size, size), jnp.bfloat16),
             pltpu.SMEM((1, levels - 1), jnp.int32),
             pltpu.VMEM((1, 128), jnp.int32),
-            pltpu.VMEM((outer, 1, 128), jnp.int32),
+            pltpu.VMEM((INNER, 1, 128), jnp.int32),
             pltpu.VMEM((levels, 8, 128), jnp.float32),
             pltpu.VMEM((levels, 8, 128), jnp.float32),
             pltpu.VMEM((levels - 1, 8, 128), jnp.bfloat16),
+            pltpu.VMEM((levels - 1, INNER, 8, 128), jnp.bfloat16),
+            pltpu.VMEM((outer, 8, 128), jnp.float32),
             pltpu.VMEM((levels - 1, outer, 8, 128), jnp.bfloat16),
-            pltpu.VMEM((INNER, 8, 128), jnp.float32),
-            pltpu.VMEM((levels - 1, INNER, 8, 128), jnp.float32),
-            pltpu.VMEM((levels - 1, INNER, 8, 128), jnp.float32),
+            pltpu.VMEM((levels - 1, outer, 8, 128), jnp.bfloat16),
             dma((2 + 3 * levels - 1,)),
+            pltpu.SemaphoreType.REGULAR((max(1, (outer // 2 - 1).bit_length()),)),
             dma, dma,
             dma((levels,)), dma((levels,)),
             dma((levels - 1,)), dma((levels - 1,)),

time: 49.1 us -> 45.5 us (0.927)
  Pallas kernels: 47.2 us -> 44.7 us
  local copies, waits for them, and re-layouts: 1.31 us -> 0.6 us
    pallas_call x1, Pallas kernels: 47.2 us -> 44.7 us  [shards(): pl.pallas_call(functools.partial(kernel, outer, groups), out_shape=pltpu....]
    unnamed x1, local copies, waits for them, and re-layouts: 1.31 us -> 0.6 us
where the time goes in v2:
time: 45.5 us; the launch traced here: 45.3 us
  Pallas kernels  44.7 us (98%)
  local copies, waits for them, and re-layouts  0.6 us (1%)
    pallas_call x1, Pallas kernels, shards(): pl.pallas_call(functools.partial(kernel, outer, groups), out_shape=pltpu....  44.7 us

profile of v2, /device:TPU:6, one launch (start us, length us, event | category | flops | bytes accessed | tf_op | source)
XLA Modules:
  0.0 45.3 jit_solution(13632372026912730085)
XLA Ops:
  0.0 44.7 %shard_map.55 = f32[3,8,128]{2,1,0:T(8,128)S(1)} custom-call(f32[3,8,128]{2,1,0:T(8,128)} %bitcast.18, bf16[3,512,512]{2,1,0:T(8,128)(2,1)} %bitcast.15, bf16[3,512,512]{2,1,0:T(8,128)(2,1)} %bitcast.16, bf16[2,512,512]{2,1,0:T(8,128)(2,1)} %bitcast.17, s32[1,2]{1,0:T(1,128)} %bitcast.19), custom_call_target="tpu_custom_call" | custom-call | tf_op jit(solution)/shard_map/pallas_call | solution.py:251
  44.7 0.6 %copy.9 = f32[3,1,1,2,512]{4,3,2,1,0:T(2,128)} copy(f32[3,1,1,2,512]{4,3,2,1,0:T(2,128)S(1)} %bitcast.14) | data formatting | bytes 24576

commit v3 on v2

--- a/solution.py
+++ b/solution.py
@@ -17,7 +17,7 @@
 
 def kernel(
     outer, groups, rhs_hbm, inverse_hbm, coupler_hbm, block_hbm, route_hbm, out_ref,
-    rhs, inverse, coupler, block, route, code, codes, solved, before, sent, yland, held, part, zland,
+    rhs, inverse, coupler, block, route, code, codes, solved, before, sent, early, relay, direct, yland, held, part, zland,
     in_sem, meet, code_send, code_recv, x_send, x_recv, y_send, y_recv, z_send, z_recv,
 ):
     levels = rhs.shape[0]
@@ -34,7 +34,8 @@
         return {"rows": zpos * INNER + (spot + offset) % INNER}
 
     barrier = pltpu.get_barrier_semaphore()
-    for offset in (1, outer - 1):
+    near = sorted({offset % outer for offset in (2, -2, 1, -1)} - {0})
+    for offset in near:
         pl.semaphore_signal(barrier, inc=1, device_id=z_peer(offset), device_id_type=MESH)
     for offset in far_first(INNER):
         pl.semaphore_signal(barrier, inc=1, device_id=y_peer(offset), device_id_type=MESH)
@@ -84,33 +85,36 @@
         p = jnp.dot(stack, matrix, preferred_element_type=jnp.float32)
         return fold(p[0:8])
 
-    def contribute(level):
-        sent[level] = rounded_product(solved[level], block[level]).astype(jnp.bfloat16)
-
-    loads[0].wait()
-    loads[1].wait()
-    both = route[0, 0] + 256 * route[0, 1]
-    code[...] = jnp.full((1, 128), both, jnp.int32)
-    matrices[0]["D"].wait()
-    for copy in loads[5:]:
-        copy.start()
-    solved[0] = product(rhs[0], inverse[0])
-    matrices[0]["E"].wait()
-    contribute(0)
-    matrices[0]["C"].wait()
-
-    pl.semaphore_wait(barrier, 2 + INNER - 1 + 1)
-
-    rounds = max(1, (outer // 2 - 1).bit_length())
+    def contribution(level):
+        return rounded_product(solved[level], block[level])
+
+    def combine(level):
+        def half(step, carry):
+            rows = pl.ds(pl.multiple_of(step * 256, 256), 256)
+            both = jnp.dot(coupler[level, rows], inverse[level], preferred_element_type=jnp.float32)
+            relay[level, rows] = both.astype(jnp.bfloat16)
+            if level < levels - 1:
+                onward = jnp.dot(relay[level, rows], block[level], preferred_element_type=jnp.float32)
+                direct[level, rows] = onward.astype(jnp.bfloat16)
+            return carry
+
+        lax.fori_loop(0, 2, half, 0)
+
+    strides, known = [], min(2, outer // 2)
+    while known < outer // 2:
+        strides.append(min(known, outer // 2 - known))
+        known += strides[-1]
 
     def greet(step):
-        for offset in (2**step, outer - 2**step):
+        for offset in sorted({strides[step], outer - strides[step]}):
             pl.semaphore_signal(meet.at[step], inc=1, device_id=z_peer(offset), device_id_type=MESH)
 
     def met(step):
-        pl.semaphore_wait(meet.at[step], 2)
-
-    greet(0)
+        pl.semaphore_wait(meet.at[step], len({strides[step], outer - strides[step]}))
+
+    pl.semaphore_wait(barrier, len(near) + INNER - 1 + 1)
+    if strides:
+        greet(0)
 
     def code_copy(offset):
         return pltpu.make_async_remote_copy(
@@ -145,65 +149,86 @@
         for offset in y_order:
             y_copy(level, offset).start()
 
-    for offset in y_order:
-        code_copy(offset).start()
-    codes[0] = code[...]
-
     def total_of(terms):
         while len(terms) > 1:
             terms = [terms[i] + terms[i + 1] for i in range(0, len(terms) - 1, 2)] + terms[len(terms) & ~1 :]
         return terms[0]
 
+    loads[0].wait()
+    matrices[0]["D"].wait()
+    for copy in loads[5:]:
+        copy.start()
+    solved[0] = product(rhs[0], inverse[0])
+
+    @pl.when(grp == 0)
+    def _():
+        x_copy(0).start()
+
+    matrices[0]["E"].wait()
+    early[0] = contribution(0)
+    loads[1].wait()
+    both = route[0, 0] + 256 * route[0, 1]
+    code[...] = jnp.full((1, 128), both, jnp.int32)
+    codes[0] = code[...]
+
+    @pl.when(grp == 0)
+    def _():
+        sent[0] = early[0].astype(jnp.bfloat16)
+        scatter(0)
+
+    for offset in y_order:
+        code_copy(offset).start()
+    if strides:
+        met(0)
+        for step in range(1, len(strides)):
+            greet(step)
+            if step < len(strides) - 1:
+                met(step)
+    matrices[0]["C"].wait()
+
+    @pl.when(grp > 0)
+    def _():
+        combine(0)
+
     for level in range(levels):
+        last = level == levels - 1
         if level > 0:
-            matrices[level]["D"].wait()
-            matrices[level]["C"].wait()
-            if level < levels - 1:
-                matrices[level]["E"].wait()
             bulk_wait(zland.at[level - 1, pl.ds(1, outer - 1)], z_recv.at[level - 1])
             incoming = total_of(
                 [part[level - 1, 0].astype(jnp.float32)]
                 + [zland[level - 1, offset].astype(jnp.float32) for offset in range(1, outer)]
             )
             solved[level] = product(rhs[level] - incoming, inverse[level])
-        else:
+
             @pl.when(grp == 0)
             def _():
-                x_copy(0).start()
-                scatter(0)
-
-            met(0)
-            if rounds > 1:
-                greet(1)
+                x_copy(level).start()
+                if not last:
+                    sent[level] = contribution(level).astype(jnp.bfloat16)
+                    scatter(level)
+
+            if not last:
+                @pl.when(grp > 0)
+                def _():
+                    early[level] = contribution(level)
 
         @pl.when(grp > 0)
         def _():
             bulk_wait(before.at[level], x_recv.at[level])
-            solved[level] = solved[level] - product(product(before[level], coupler[level]), inverse[level])
+            prior = before[level]
+            solved[level] = solved[level] - product(prior, relay[level])
 
             @pl.when(grp < groups - 1)
             def _():
                 x_copy(level).start()
 
-            if level == 0:
-                contribute(0)
-                scatter(0)
-
-        if level > 0:
-            @pl.when(grp == 0)
-            def _():
-                x_copy(level).start()
-
-        if level == levels - 1:
+            if not last:
+                sent[level] = (early[level] - product(prior, direct[level])).astype(jnp.bfloat16)
+                scatter(level)
+
+        if last:
             break
-        if level > 0:
-            contribute(level)
-            scatter(level)
-        else:
-            for step in range(1, rounds):
-                met(step)
-                if step + 1 < rounds:
-                    greet(step + 1)
+        if level == 0:
             bulk_wait(codes.at[pl.ds(1, INNER - 1)], code_recv)
         bulk_wait(yland.at[level, pl.ds(1, INNER - 1)], y_recv.at[level])
 
@@ -221,11 +246,20 @@
             if level > 0:
                 total = total + held[offset]
             part[level, offset] = total.astype(jnp.bfloat16)
+            if level == 0 and len(strides) > 1 and offset == z_order[0]:
+                met(len(strides) - 1)
             if offset:
                 z_copy(level, offset).start()
         if level == 0:
             for offset in range(outer):
                 held[offset] = gathered(((zpos + offset) % outer) * INNER + spot + rowblocks)
+            for copy in loads[5:]:
+                copy.wait()
+
+            @pl.when(grp > 0)
+            def _():
+                for later in range(1, levels):
+                    combine(later)
 
     out_ref[...] = solved[...]
 
@@ -264,12 +298,15 @@
             pltpu.VMEM((levels, 8, 128), jnp.float32),
             pltpu.VMEM((levels, 8, 128), jnp.float32),
             pltpu.VMEM((levels - 1, 8, 128), jnp.bfloat16),
+            pltpu.VMEM((levels - 1, 8, 128), jnp.float32),
+            pltpu.VMEM((levels, size, size), jnp.bfloat16),
+            pltpu.VMEM((levels - 1, size, size), jnp.bfloat16),
             pltpu.VMEM((levels - 1, INNER, 8, 128), jnp.bfloat16),
             pltpu.VMEM((outer, 8, 128), jnp.float32),
             pltpu.VMEM((levels - 1, outer, 8, 128), jnp.bfloat16),
             pltpu.VMEM((levels - 1, outer, 8, 128), jnp.bfloat16),
             dma((2 + 3 * levels - 1,)),
-            pltpu.SemaphoreType.REGULAR((max(1, (outer // 2 - 1).bit_length()),)),
+            pltpu.SemaphoreType.REGULAR((max(1, outer.bit_length() - 2),)),
             dma, dma,
             dma((levels,)), dma((levels,)),
             dma((levels - 1,)), dma((levels - 1,)),

time: 45.5 us -> 43.4 us (0.954)
  Pallas kernels: 44.7 us -> 42.7 us
    pallas_call x1, Pallas kernels: 44.7 us -> 42.7 us  [shards(): pl.pallas_call(functools.partial(kernel, outer, groups), out_shape=pltpu....]
where the time goes in v3:
time: 43.4 us; the launch traced here: 43.3 us
  Pallas kernels  42.7 us (98%)
  local copies, waits for them, and re-layouts  0.6 us (1%)
    pallas_call x1, Pallas kernels, shards(): pl.pallas_call(functools.partial(kernel, outer, groups), out_shape=pltpu....  42.7 us

profile of v3, /device:TPU:6, one launch (start us, length us, event | category | flops | bytes accessed | tf_op | source)
XLA Modules:
  0.0 43.3 jit_solution(13844903381624191067)
XLA Ops:
  0.0 42.7 %shard_map.55 = f32[3,8,128]{2,1,0:T(8,128)S(1)} custom-call(f32[3,8,128]{2,1,0:T(8,128)} %bitcast.18, bf16[3,512,512]{2,1,0:T(8,128)(2,1)} %bitcast.15, bf16[3,512,512]{2,1,0:T(8,128)(2,1)} %bitcast.16, bf16[2,512,512]{2,1,0:T(8,128)(2,1)} %bitcast.17, s32[1,2]{1,0:T(1,128)} %bitcast.19), custom_call_target="tpu_custom_call" | custom-call | tf_op jit(solution)/shard_map/pallas_call | solution.py:285
  42.7 0.6 %copy.9 = f32[3,1,1,2,512]{4,3,2,1,0:T(2,128)} copy(f32[3,1,1,2,512]{4,3,2,1,0:T(2,128)S(1)} %bitcast.14) | data formatting | bytes 24576

commit v4 on v3

--- a/solution.py
+++ b/solution.py
@@ -34,7 +34,7 @@
         return {"rows": zpos * INNER + (spot + offset) % INNER}
 
     barrier = pltpu.get_barrier_semaphore()
-    near = sorted({offset % outer for offset in (2, -2, 1, -1)} - {0})
+    near = sorted({offset % outer for offset in (4, -4, 3, -3, 2, -2, 1, -1)} - {0}, key=lambda offset: -min(offset, outer - offset))
     for offset in near:
         pl.semaphore_signal(barrier, inc=1, device_id=z_peer(offset), device_id_type=MESH)
     for offset in far_first(INNER):
@@ -100,7 +100,7 @@
 
         lax.fori_loop(0, 2, half, 0)
 
-    strides, known = [], min(2, outer // 2)
+    strides, known = [], min(4, outer // 2)
     while known < outer // 2:
         strides.append(min(known, outer // 2 - known))
         known += strides[-1]
@@ -176,14 +176,14 @@
         sent[0] = early[0].astype(jnp.bfloat16)
         scatter(0)
 
-    for offset in y_order:
-        code_copy(offset).start()
-    if strides:
+    if len(strides) > 1:
         met(0)
         for step in range(1, len(strides)):
             greet(step)
             if step < len(strides) - 1:
                 met(step)
+    for offset in y_order:
+        code_copy(offset).start()
     matrices[0]["C"].wait()
 
     @pl.when(grp > 0)
@@ -212,19 +212,27 @@
                 def _():
                     early[level] = contribution(level)
 
-        @pl.when(grp > 0)
+        def absorb():
+            solved[level] = solved[level] - product(before[level], relay[level])
+
+        def pass_on():
+            sent[level] = (early[level] - product(before[level], direct[level])).astype(jnp.bfloat16)
+            scatter(level)
+
+        @pl.when((grp > 0) & (grp < groups - 1))
         def _():
             bulk_wait(before.at[level], x_recv.at[level])
-            prior = before[level]
-            solved[level] = solved[level] - product(prior, relay[level])
-
-            @pl.when(grp < groups - 1)
-            def _():
-                x_copy(level).start()
-
+            absorb()
+            x_copy(level).start()
             if not last:
-                sent[level] = (early[level] - product(prior, direct[level])).astype(jnp.bfloat16)
-                scatter(level)
+                pass_on()
+
+        @pl.when(grp == groups - 1)
+        def _():
+            bulk_wait(before.at[level], x_recv.at[level])
+            if not last:
+                pass_on()
+            absorb()
 
         if last:
             break
@@ -246,7 +254,7 @@
             if level > 0:
                 total = total + held[offset]
             part[level, offset] = total.astype(jnp.bfloat16)
-            if level == 0 and len(strides) > 1 and offset == z_order[0]:
+            if level == 0 and strides and offset == z_order[0]:
                 met(len(strides) - 1)
             if offset:
                 z_copy(level, offset).start()

time: 43.4 us -> 42.8 us (0.986)
  Pallas kernels: 42.7 us -> 42.1 us
    pallas_call x1, Pallas kernels: 42.7 us -> 42.1 us  [shards(): pl.pallas_call(functools.partial(kernel, outer, groups), out_shape=pltpu....]
where the time goes in v4:
time: 42.8 us; the launch traced here: 42.7 us
  Pallas kernels  42.1 us (98%)
  local copies, waits for them, and re-layouts  0.6 us (1%)
    pallas_call x1, Pallas kernels, shards(): pl.pallas_call(functools.partial(kernel, outer, groups), out_shape=pltpu....  42.1 us

profile of v4, /device:TPU:6, one launch (start us, length us, event | category | flops | bytes accessed | tf_op | source)
XLA Modules:
  0.0 42.7 jit_solution(7861960921726090782)
XLA Ops:
  0.0 42.1 %shard_map.55 = f32[3,8,128]{2,1,0:T(8,128)S(1)} custom-call(f32[3,8,128]{2,1,0:T(8,128)} %bitcast.18, bf16[3,512,512]{2,1,0:T(8,128)(2,1)} %bitcast.15, bf16[3,512,512]{2,1,0:T(8,128)(2,1)} %bitcast.16, bf16[2,512,512]{2,1,0:T(8,128)(2,1)} %bitcast.17, s32[1,2]{1,0:T(1,128)} %bitcast.19), custom_call_target="tpu_custom_call" | custom-call | tf_op jit(solution)/shard_map/pallas_call | solution.py:293
  42.1 0.6 %copy.9 = f32[3,1,1,2,512]{4,3,2,1,0:T(2,128)} copy(f32[3,1,1,2,512]{4,3,2,1,0:T(2,128)S(1)} %bitcast.14) | data formatting | bytes 24576

commit v5 on v4

--- a/solution.py
+++ b/solution.py
@@ -112,10 +112,6 @@
     def met(step):
         pl.semaphore_wait(meet.at[step], len({strides[step], outer - strides[step]}))
 
-    pl.semaphore_wait(barrier, len(near) + INNER - 1 + 1)
-    if strides:
-        greet(0)
-
     def code_copy(offset):
         return pltpu.make_async_remote_copy(
             src_ref=code, dst_ref=codes.at[offset], send_sem=code_send, recv_sem=code_recv,
@@ -159,21 +155,27 @@
     for copy in loads[5:]:
         copy.start()
     solved[0] = product(rhs[0], inverse[0])
-
-    @pl.when(grp == 0)
-    def _():
-        x_copy(0).start()
-
-    matrices[0]["E"].wait()
-    early[0] = contribution(0)
     loads[1].wait()
     both = route[0, 0] + 256 * route[0, 1]
     code[...] = jnp.full((1, 128), both, jnp.int32)
     codes[0] = code[...]
+    matrices[0]["E"].wait()
+    early[0] = contribution(0)
+    sent[0] = early[0].astype(jnp.bfloat16)
+
+    pl.semaphore_wait(barrier, len(near) + INNER - 1 + 1)
+    if strides:
+        greet(0)
 
     @pl.when(grp == 0)
     def _():
-        sent[0] = early[0].astype(jnp.bfloat16)
+        x_copy(0).start()
+
+    for offset in y_order:
+        code_copy(offset).start()
+
+    @pl.when(grp == 0)
+    def _():
         scatter(0)
 
     if len(strides) > 1:
@@ -182,8 +184,6 @@
             greet(step)
             if step < len(strides) - 1:
                 met(step)
-    for offset in y_order:
-        code_copy(offset).start()
     matrices[0]["C"].wait()
 
     @pl.when(grp > 0)

time: 42.8 us -> 42.8 us (level)
  no operation moved by 1% of the time
where the time goes in v5:
time: 42.8 us; the launch traced here: 42.6 us
  Pallas kernels  42 us (98%)
  local copies, waits for them, and re-layouts  0.6 us (1%)
    pallas_call x1, Pallas kernels, shards(): pl.pallas_call(functools.partial(kernel, outer, groups), out_shape=pltpu....  42 us

profile of v5, /device:TPU:6, one launch (start us, length us, event | category | flops | bytes accessed | tf_op | source)
XLA Modules:
  0.0 42.6 jit_solution(12170545008078774497)
XLA Ops:
  0.0 42.0 %shard_map.55 = f32[3,8,128]{2,1,0:T(8,128)S(1)} custom-call(f32[3,8,128]{2,1,0:T(8,128)} %bitcast.18, bf16[3,512,512]{2,1,0:T(8,128)(2,1)} %bitcast.15, bf16[3,512,512]{2,1,0:T(8,128)(2,1)} %bitcast.16, bf16[2,512,512]{2,1,0:T(8,128)(2,1)} %bitcast.17, s32[1,2]{1,0:T(1,128)} %bitcast.19), custom_call_target="tpu_custom_call" | custom-call | tf_op jit(solution)/shard_map/pallas_call | solution.py:293
  42.0 0.6 %copy.9 = f32[3,1,1,2,512]{4,3,2,1,0:T(2,128)} copy(f32[3,1,1,2,512]{4,3,2,1,0:T(2,128)S(1)} %bitcast.14) | data formatting | bytes 24576

commit v6 on v5

--- a/solution.py
+++ b/solution.py
@@ -169,14 +169,14 @@
 
     @pl.when(grp == 0)
     def _():
-        x_copy(0).start()
+        scatter(0)
 
     for offset in y_order:
         code_copy(offset).start()
 
     @pl.when(grp == 0)
     def _():
-        scatter(0)
+        x_copy(0).start()
 
     if len(strides) > 1:
         met(0)

time: 42.8 us -> 42.8 us (level)
  no operation moved by 1% of the time
where the time goes in v6:
time: 42.8 us; the launch traced here: 42.6 us
  Pallas kernels  42 us (98%)
  local copies, waits for them, and re-layouts  0.6 us (1%)
    pallas_call x1, Pallas kernels, shards(): pl.pallas_call(functools.partial(kernel, outer, groups), out_shape=pltpu....  42 us

profile of v6, /device:TPU:6, one launch (start us, length us, event | category | flops | bytes accessed | tf_op | source)
XLA Modules:
  0.0 42.6 jit_solution(5279193210732811825)
XLA Ops:
  0.0 42.0 %shard_map.55 = f32[3,8,128]{2,1,0:T(8,128)S(1)} custom-call(f32[3,8,128]{2,1,0:T(8,128)} %bitcast.18, bf16[3,512,512]{2,1,0:T(8,128)(2,1)} %bitcast.15, bf16[3,512,512]{2,1,0:T(8,128)(2,1)} %bitcast.16, bf16[2,512,512]{2,1,0:T(8,128)(2,1)} %bitcast.17, s32[1,2]{1,0:T(1,128)} %bitcast.19), custom_call_target="tpu_custom_call" | custom-call | tf_op jit(solution)/shard_map/pallas_call | solution.py:293
  42.0 0.6 %copy.9 = f32[3,1,1,2,512]{4,3,2,1,0:T(2,128)} copy(f32[3,1,1,2,512]{4,3,2,1,0:T(2,128)S(1)} %bitcast.14) | data formatting | bytes 24576
